TPU v7x, 256 devices: a whole 4x4x8 slice. The times are simulated.
256 devices in a mesh: px: 4 (over z_lo), py: 8 (over y, core), ch: 8 (over z_hi, x).
Axes of the slice: x: 4, y: 4, z: 8 (z_hi: 2, z_lo: 4; z = z_hi * 4 + z_lo), core: 2. Of those that a mesh axis runs over, the one named last changes fastest.
Arguments:
- features: bfloat16 [128, 12, 8, 4, 512], P('ch', None, 'py', 'px'), may hold values from -6 to 6
- cotangent: bfloat16 [128, 12, 8, 4, 512], P('ch', None, 'py', 'px'), may hold values from -6 to 6
- weight: bfloat16 [3, 3, 128, 128], replicated, may hold values from -0.1875 to 0.1875
- edge_table: int32 [12, 4, 3], replicated, may hold values from 0 to 11, as said below
- corner_table: int32 [12, 4, 2], replicated, may hold values from 0 to 11, as said below
Outputs:
- activation: bfloat16 [128, 12, 8, 4, 512], P('ch', None, 'py', 'px')
- input_grad: bfloat16 [128, 12, 8, 4, 512], P('ch', None, 'py', 'px')
Inputs may be any that keep to these rules, and one draw needn't show every extreme that they name: edge_table[f, e] = (g, s, r): beyond edge e of face f lie the pixels of side s of face g, in reverse order if r = 1; every side of every face is named exactly once, and if (f, e) names (g, s) then (g, s) names (f, e) with the same r. corner_table[f, c] = (h, q): corner c of face f takes corner pixel q of face h; in each corner column every face appears once, and each q appears 12 times.
All inputs are finite; a program needn't handle non-finite values.
Results may differ from a plain program's by a relative error of at most 0.0049.
Values may be sent and summed in bfloat16 or wider, within the bound.
A program may use at most 192 MiB of HBM per device.

v0:
```python
import jax
import jax.numpy as jnp
from jax import lax
from jax.sharding import PartitionSpec as P

RB = 32


def with_halo(array, sides, width):
    for axis, dim in sides:
        size, length = (lax.axis_size(axis), array.shape[dim])
        up = [(i, (i + 1) % size) for i in range(size - 1)]
        down = [(j, i) for i, j in up]
        last = lax.slice_in_dim(array, length - width, length, axis=dim)
        leading = lax.slice_in_dim(array, 0, width, axis=dim)
        before = lax.ppermute(last, axis, up)
        after = lax.ppermute(leading, axis, down)
        array = jnp.concatenate([before, array, after], axis=dim)
    return array


def edge_strips(lines, edge_table, corner_table):
    chan_count = lines.shape[0]
    face_count = lines.shape[1]
    side_len = lines.shape[3]
    flat_lines = lines.reshape(chan_count, face_count * 4, side_len)
    pixels = jnp.stack(
        [lines[:, :, 0, 0], lines[:, :, 0, -1], lines[:, :, 1, 0], lines[:, :, 1, -1]], axis=2
    ).reshape(chan_count, face_count * 4)
    corner_index = corner_table[:, :, 0] * 4 + corner_table[:, :, 1]
    corner_vals = jnp.take(pixels, corner_index, axis=1)
    strips = []
    for edge_num, start_corner, end_corner in ((0, 0, 1), (1, 2, 3), (2, 0, 2), (3, 1, 3)):
        source_row = edge_table[:, edge_num, 0] * 4 + edge_table[:, edge_num, 1]
        strip_line = jnp.take(flat_lines, source_row, axis=1)
        flipped = (edge_table[:, edge_num, 2] == 1)[None, :, None]
        strip_line = jnp.where(flipped, strip_line[:, :, ::-1], strip_line)
        strips.append(
            jnp.concatenate(
                [
                    corner_vals[:, :, start_corner : start_corner + 1],
                    strip_line,
                    corner_vals[:, :, end_corner : end_corner + 1],
                ],
                axis=2,
            )
        )
    return strips


def face_lines_of(field, row_pos, col_pos, px_count, py_count):
    chan_block = field.shape[0]
    face_count = field.shape[1]
    col_len = field.shape[2]
    row_len = field.shape[3]
    side_len = row_len * px_count
    blank = jnp.zeros((chan_block, face_count, side_len), jnp.float32)

    def placed(values, offset, active):
        return jnp.where(
            active,
            lax.dynamic_update_slice_in_dim(blank, values.astype(jnp.float32), offset, 2),
            0.0,
        )

    contrib = jnp.stack(
        [
            placed(field[:, :, 0, :], row_pos * row_len, col_pos == 0),
            placed(field[:, :, -1, :], row_pos * row_len, col_pos == py_count - 1),
            placed(field[:, :, :, 0], col_pos * col_len, row_pos == 0),
            placed(field[:, :, :, -1], col_pos * col_len, row_pos == px_count - 1),
        ],
        axis=2,
    )
    return lax.psum(contrib.astype(jnp.bfloat16), ("px", "py"))


def pad_field(field, edge_table, corner_table):
    col_len = field.shape[2]
    row_len = field.shape[3]
    row_pos = lax.axis_index("px")
    col_pos = lax.axis_index("py")
    px_count = lax.axis_size("px")
    py_count = lax.axis_size("py")
    padded = with_halo(field, (("px", 3), ("py", 2)), 1)
    lines = face_lines_of(field, row_pos, col_pos, px_count, py_count)
    strips = edge_strips(lines, edge_table, corner_table)
    top_row = lax.dynamic_slice_in_dim(strips[0], row_pos * row_len, row_len + 2, 2)
    bottom_row = lax.dynamic_slice_in_dim(strips[1], row_pos * row_len, row_len + 2, 2)
    left_col = lax.dynamic_slice_in_dim(strips[2], col_pos * col_len, col_len + 2, 2)
    right_col = lax.dynamic_slice_in_dim(strips[3], col_pos * col_len, col_len + 2, 2)
    padded = padded.at[:, :, 0, :].set(jnp.where(col_pos == 0, top_row, padded[:, :, 0, :]))
    padded = padded.at[:, :, -1, :].set(
        jnp.where(col_pos == py_count - 1, bottom_row, padded[:, :, -1, :])
    )
    padded = padded.at[:, :, :, 0].set(jnp.where(row_pos == 0, left_col, padded[:, :, :, 0]))
    padded = padded.at[:, :, :, -1].set(
        jnp.where(row_pos == px_count - 1, right_col, padded[:, :, :, -1])
    )
    return padded


def forward_taps(padded, taps, out_cols, out_rows):
    summed = None
    for tap_row in range(3):
        for tap_col in range(3):
            window = padded[:, :, tap_row : tap_row + out_cols, tap_col : tap_col + out_rows]
            term_val = jnp.einsum(
                "oc,cfab->ofab", taps[tap_row, tap_col], window, preferred_element_type=jnp.float32
            )
            summed = term_val if summed is None else summed + term_val
    return summed


def backward_taps(padded, taps, out_cols, out_rows):
    summed = None
    for tap_row in range(3):
        for tap_col in range(3):
            window = padded[
                :, :, 2 - tap_row : 2 - tap_row + out_cols, 2 - tap_col : 2 - tap_col + out_rows
            ]
            term_val = jnp.einsum(
                "oc,ofab->cfab", taps[tap_row, tap_col], window, preferred_element_type=jnp.float32
            )
            summed = term_val if summed is None else summed + term_val
    return summed


def gate_outputs(preact, cotangent):
    sigmoid_val = jax.nn.sigmoid(preact)
    activation = (preact * sigmoid_val).astype(jnp.bfloat16)
    gated = (
        cotangent.astype(jnp.float32) * sigmoid_val * (1.0 + preact * (1.0 - sigmoid_val))
    ).astype(jnp.bfloat16)
    return (activation, gated)


def local(features, cotangent, weight, edge_table, corner_table):
    chan_block = features.shape[0]
    face_count = features.shape[1]
    tile_len = features.shape[4]
    row_len = RB
    col_len = tile_len // row_len
    features = features.reshape(chan_block, face_count, col_len, row_len)
    cotangent = cotangent.reshape(chan_block, face_count, col_len, row_len)
    ch_pos = lax.axis_index("ch")
    feat_pad = pad_field(features, edge_table, corner_table)
    own_taps = lax.dynamic_slice_in_dim(weight, ch_pos * chan_block, chan_block, 2)
    piece_taps = own_taps
    preact = forward_taps(
        lax.all_gather(feat_pad, "ch", axis=0, tiled=True), piece_taps, col_len, row_len
    )
    activation, gated = gate_outputs(preact, cotangent)
    grad_pad = pad_field(gated, edge_table, corner_table)
    input_taps = lax.dynamic_slice_in_dim(weight, ch_pos * chan_block, chan_block, 3)
    piece_taps = input_taps
    input_grad = backward_taps(
        lax.all_gather(grad_pad, "ch", axis=0, tiled=True), piece_taps, col_len, row_len
    ).astype(jnp.bfloat16)
    out_shape = (chan_block, face_count, 1, 1, tile_len)
    return (activation.reshape(out_shape), input_grad.reshape(out_shape))


def solution(mesh):
    return jax.shard_map(
        local,
        mesh=mesh,
        in_specs=(P("ch", None, "py", "px", None), P("ch", None, "py", "px", None), P(), P(), P()),
        out_specs=(P("ch", None, "py", "px", None), P("ch", None, "py", "px", None)),
        check_vma=False,
    )
```

profile of v0, /device:TPU:8, one launch (start us, length us, event | category | flops | bytes accessed | tf_op | source)
XLA Modules:
  0.0 1055.1 jit_solution(10775510683861696942)
XLA Ops:
  11.2 3.0 copy.696
  16.1 2.7 select_n.196
  18.7 2.7 select_n.200
  23.1 2.6 copy.698
  27.0 7.1 collective-permute-start
  43.6 1.9 collective-permute-start.2
  45.5 3.9 collective-permute-start.3
  53.1 254.8 %all-reduce.3.cloned.1.call-done = bf16[16,12,4,128]{1,0,3,2:T(8,128)(2,1)} async-done(((bf16[16,12,4,128]{1,0,3,2:T(8,128)(2,1)}), bf16[16,12,4,128]{1,0,3,2:T(8,128)(2,1)}) %all-reduce.3.cloned.1.call-update) | async-done | bytes 196624 | tf_op jit(solution)/shard_map/psum | solution.py:75
  307.9 3.0 copy.702
  318.9 3.8 scatter.30
  326.8 18.3 %scatter.31 = bf16[16,12,18,34]{3,0,2,1:T(8,128)(2,1)S(1)} dynamic-update-slice(bf16[16,12,18,34]{3,0,2,1:T(8,128)(2,1)S(1)} %scatter.30, bf16[16,12,18,1]{3,0,2,1:T(8,128)(2,1)S(1)} %copy.707, s32[]{:T(128)} %constant.235.clone.1, s32[]{:T(128)} %constant.235.clone.1, s32[]{:T(128)} %constant.235.clone.1, s32[]{:T(128)} %constant.249.clone.1) | dynamic-update-slice | bytes 13828 | tf_op jit(solution)/shard_map/scatter | solution.py:97
  347.9 162.8 %all-gather.3.cloned.1.call-done = bf16[128,12,18,34]{3,0,2,1:T(8,128)(2,1)} async-done(((bf16[16,12,18,34]{3,0,2,1:T(8,128)(2,1)}), bf16[128,12,18,34]{3,0,2,1:T(8,128)(2,1)}) %all-gather.3.cloned.1.call-update) | async-done | bytes 1880080 | tf_op jit(solution)/shard_map/all_gather | solution.py:151
  510.7 4.7 fusion.20
  524.6 2.0 fusion.18
  526.6 2.6 fusion.37
  531.6 2.3 copy.725
  536.3 2.2 collective-permute-start.4
  541.1 1.9 select_n.220
  543.0 1.9 select_n.223
  545.7 2.6 copy.727
  551.1 1.9 collective-permute-start.6
  553.0 3.9 collective-permute-start.7
  559.2 266.2 %all-reduce.5.cloned.1.call-done = bf16[16,12,4,128]{1,0,3,2:T(8,128)(2,1)} async-done(((bf16[16,12,4,128]{1,0,3,2:T(8,128)(2,1)}), bf16[16,12,4,128]{1,0,3,2:T(8,128)(2,1)}) %all-reduce.5.cloned.1.call-update) | async-done | bytes 196624 | tf_op jit(solution)/shard_map/psum | solution.py:75
  825.4 3.0 copy.731
  837.1 3.8 scatter.36
  844.2 18.6 %scatter.39 = bf16[16,12,18,34]{3,0,2,1:T(8,128)(2,1)S(1)} dynamic-update-slice(bf16[16,12,18,34]{3,0,2,1:T(8,128)(2,1)S(1)} %scatter.36, bf16[16,12,18,1]{3,0,2,1:T(8,128)(2,1)S(1)} %copy.735, s32[]{:T(128)} %constant.235.clone.1, s32[]{:T(128)} %constant.235.clone.1, s32[]{:T(128)} %constant.235.clone.1, s32[]{:T(128)} %constant.249.clone.1) | dynamic-update-slice | bytes 13828 | tf_op jit(solution)/shard_map/scatter | solution.py:97
  865.5 162.9 %all-gather.5.cloned.1.call-done = bf16[128,12,18,34]{3,0,2,1:T(8,128)(2,1)} async-done(((bf16[16,12,18,34]{3,0,2,1:T(8,128)(2,1)}), bf16[128,12,18,34]{3,0,2,1:T(8,128)(2,1)}) %all-gather.5.cloned.1.call-update) | async-done | bytes 1880080 | tf_op jit(solution)/shard_map/all_gather | solution.py:158
  1028.4 4.8 fusion.2
  1034.3 1.9 fusion.10
  1037.2 1.9 fusion.14
  1040.9 1.9 fusion.8
  1044.1 2.3 add_convert_fusion
  (201 shorter events, 80.0 us)
Async XLA Ops:
  7.2 503.6 %copy-start = (bf16[3,3,128,128]{3,2,1,0:T(8,128)(2,1)S(1)}, bf16[3,3,128,128]{3,2,1,0:T(8,128)(2,1)}, u32[]{:S(2)}) copy-start(bf16[3,3,128,128]{3,2,1,0:T(8,128)(2,1)} %param.27) | copy-start | bytes 884740
  7.2 300.8 %all-reduce.3.cloned.1.call-start = ((), (), s32[]{:S(2)}) async-start(), calls=%async_computation | async-start | bytes 4194304 | tf_op jit(solution)/shard_map/psum | solution.py:75
  25.7 10.9 %copy-start.17 = (s32[12,4,3]{0,1,2:T(4,128)S(1)}, s32[12,4,3]{0,1,2:T(4,128)}, u32[]{:S(2)}) copy-start(s32[12,4,3]{0,1,2:T(4,128)} %param.28) | copy-start | bytes 1732
  25.7 12.0 %copy-start.26 = (s32[12,4,2]{0,2,1:T(2,128)S(1)}, s32[12,4,2]{0,2,1:T(2,128)}, u32[]{:S(2)}) copy-start(s32[12,4,2]{0,2,1:T(2,128)} %param.29) | copy-start | bytes 1156
  25.7 485.0 %all-gather.3.cloned.1.call-start = ((), (), s32[]{:S(2)}) async-start(), calls=%async_computation.1 | async-start | bytes 7962624 | tf_op jit(solution)/shard_map/all_gather | solution.py:151
  27.0 12.3 %collective-permute-start = (bf16[16,12,16,1]{2,0,3,1:T(8,128)(2,1)S(1)}, bf16[16,12,16,1]{2,0,3,1:T(8,128)(2,1)S(1)}, u32[]{:S(2)}, u32[]{:S(2)}) collective-permute-start(bf16[16,12,16,1]{2,0,3,1:T(8,128)(2,1)S(1)} %copy.684), channel_id=1, source_target_pairs={{0,64},{64,128},{128,192},{1,65},{65,129},{129,193},{2,66},{66,130... | collective-permute-start | bytes 18440 | tf_op jit(solution)/shard_map/ppermute | solution.py:16
  35.3 6.0 collective-permute-start.1
  43.6 5.9 collective-permute-start.2
  45.5 5.4 collective-permute-start.3
  53.1 258.7 %copy-start.15 = (pred[12]{0:T(512)(128)(4,1)S(1)}, pred[12]{0:T(512)(128)(4,1)}, u32[]{:S(2)}) copy-start(pred[12]{0:T(512)(128)(4,1)} %get-tuple-element.166) | copy-start | bytes 40
  53.1 259.6 %copy-start.13 = (pred[12]{0:T(512)(128)(4,1)S(1)}, pred[12]{0:T(512)(128)(4,1)}, u32[]{:S(2)}) copy-start(pred[12]{0:T(512)(128)(4,1)} %get-tuple-element.164) | copy-start | bytes 40
  311.0 4.6 copy-start.20
  311.0 4.7 copy-start.11
  311.0 4.9 copy-start.22
  313.8 3.6 copy-start.24
  346.1 479.3 %all-reduce.5.cloned.1.call-start = ((), (), s32[]{:S(2)}) async-start(), calls=%async_computation.2 | async-start | bytes 4194304 | tf_op jit(solution)/shard_map/psum | solution.py:75
  510.7 4.8 copy-start.2
  535.1 9.9 copy-start.7
  535.1 10.2 copy-start.6
  536.3 12.1 %collective-permute-start.4 = (bf16[16,12,16,1]{2,0,3,1:T(8,128)(2,1)S(1)}, bf16[16,12,16,1]{2,0,3,1:T(8,128)(2,1)S(1)}, u32[]{:S(2)}, u32[]{:S(2)}) collective-permute-start(bf16[16,12,16,1]{2,0,3,1:T(8,128)(2,1)S(1)} %copy.720), channel_id=1, source_target_pairs={{0,64},{64,128},{128,192},{1,65},{65,129},{129,193},{2,66},{66,130... | collective-permute-start | bytes 18440 | tf_op jit(solution)/shard_map/ppermute | solution.py:16
  539.8 9.9 collective-permute-start.5
  548.4 480.1 %all-gather.5.cloned.1.call-start = ((), (), s32[]{:S(2)}) async-start(), calls=%async_computation.3 | async-start | bytes 7962624 | tf_op jit(solution)/shard_map/all_gather | solution.py:158
  551.1 5.8 collective-permute-start.6
  553.0 5.4 collective-permute-start.7
  559.1 272.2 %copy-start.16 = (pred[12]{0:T(512)(128)(4,1)S(1)}, pred[12]{0:T(512)(128)(4,1)}, u32[]{:S(2)}) copy-start(pred[12]{0:T(512)(128)(4,1)} %get-tuple-element.166) | copy-start | bytes 40
  559.2 272.4 %copy-start.25 = (pred[12]{0:T(512)(128)(4,1)S(1)}, pred[12]{0:T(512)(128)(4,1)}, u32[]{:S(2)}) copy-start(pred[12]{0:T(512)(128)(4,1)} %get-tuple-element.162) | copy-start | bytes 40
  559.2 272.5 %copy-start.14 = (pred[12]{0:T(512)(128)(4,1)S(1)}, pred[12]{0:T(512)(128)(4,1)}, u32[]{:S(2)}) copy-start(pred[12]{0:T(512)(128)(4,1)} %get-tuple-element.164) | copy-start | bytes 40
  559.2 272.7 %copy-start.23 = (pred[12]{0:T(512)(128)(4,1)S(1)}, pred[12]{0:T(512)(128)(4,1)}, u32[]{:S(2)}) copy-start(pred[12]{0:T(512)(128)(4,1)} %get-tuple-element.161) | copy-start | bytes 40
  828.4 5.5 copy-start.21
  828.5 5.6 copy-start.9
  842.9 20.9 %copy-start.5 = (bf16[16,12,16,32]{3,0,2,1:T(8,128)(2,1)S(1)}, bf16[16,12,16,32]{3,0,2,1:T(8,128)(2,1)}, u32[]{:S(2)}) copy-start(bf16[16,12,16,32]{3,0,2,1:T(8,128)(2,1)} %get-tuple-element.139) | copy-start | bytes 589828
  1028.4 4.8 copy-start.1
  (7 other events, 9.8 us)
Sparse Core Ops, SparseCore 0:
  25.8 282.0 all-reduce.2
  346.2 164.4 all-gather.2
  548.5 276.8 all-reduce.4
  863.9 164.4 all-gather.4
where the time goes:
time: 1060 us
  waiting for transfers between devices  850 us (80%)
  local copies, waits for them, and re-layouts  117 us (11%)
  matrix products  36.3 us (3%)
  starting transfers between devices  24 us (2%)
  between operations  15.2 us (1%)
  other arithmetic  12.9 us (1%)
    psum x2, waiting for transfers between devices, face_lines_of(): return lax.psum(contrib.astype(jnp.bfloat16), ('px', 'py'))  521 us
    all_gather x1, waiting for transfers between devices, local(): lax.all_gather(grad_pad, 'ch', axis=0, tiled=True)  163 us
    all_gather x1, waiting for transfers between devices, local(): lax.all_gather(feat_pad, 'ch', axis=0, tiled=True)  163 us
    scatter x2, local copies, waits for them, and re-layouts, pad_field(): padded.at[:, :, :, -1]  36.9 us
  transfers between devices with their start and end apart: 12, of which 7 were waited for; matrix products, arithmetic and copies ran while one was open for 2% of the time, Pallas kernels for 0%

commit v1 on v0

--- a/solution.py
+++ b/solution.py
@@ -72,7 +72,7 @@
         ],
         axis=2,
     )
-    return lax.psum(contrib.astype(jnp.bfloat16), ("px", "py"))
+    return lax.psum(lax.psum(contrib.astype(jnp.bfloat16), "px"), "py")
 
 
 def pad_field(field, edge_table, corner_table):

time: 1060 us -> 837 us (0.79)
  waiting for transfers between devices: 850 us -> 617 us
    psum x2 -> x4, waiting for transfers between devices: 521 us -> 289 us  [face_lines_of(): return lax.psum(lax.psum(contrib.astype(jnp.bfloat16), 'px'), 'py')]
  transfers between devices with their start and end apart: 12 -> 14, of which waited for: 7 -> 8; matrix products, arithmetic and copies ran while one was open for 2% -> 2% of each run, Pallas kernels for 0% -> 0%
where the time goes in v1:
time: 837 us; the launch traced here: 829 us
  waiting for transfers between devices  617 us (74%)
  local copies, waits for them, and re-layouts  119 us (14%)
  matrix products  36.3 us (4%)
  starting transfers between devices  27.3 us (3%)
  between operations  15.6 us (2%)
  other arithmetic  13.7 us (2%)
    psum x4, waiting for transfers between devices, face_lines_of(): return lax.psum(lax.psum(contrib.astype(jnp.bfloat16), 'px'), 'py')  289 us
    all_gather x1, waiting for transfers between devices, local(): lax.all_gather(feat_pad, 'ch', axis=0, tiled=True)  162 us
    all_gather x1, waiting for transfers between devices, local(): lax.all_gather(grad_pad, 'ch', axis=0, tiled=True)  160 us
    scatter x2, local copies, waits for them, and re-layouts, pad_field(): padded.at[:, :, :, -1]  36.9 us
    select_n x12, local copies, waits for them, and re-layouts, placed(): jnp.where(active, lax.dynamic_update_slice_in_dim(blank, values.astype(jn...  20.3 us
    dot_general x9, matrix products, forward_taps(): jnp.einsum('oc,cfab->ofab', taps[tap_row, tap_col], window, preferred_ele...  18.4 us
    dot_general x9, matrix products, backward_taps(): jnp.einsum('oc,ofab->cfab', taps[tap_row, tap_col], window, preferred_ele...  17.9 us
  transfers between devices with their start and end apart: 14, of which 8 were waited for; matrix products, arithmetic and copies ran while one was open for 2% of the time, Pallas kernels for 0%

profile of v1, /device:TPU:8, one launch (start us, length us, event | category | flops | bytes accessed | tf_op | source)
XLA Modules:
  0.0 828.6 jit_solution(11564096324096771008)
XLA Ops:
  11.2 3.0 copy.696
  16.0 2.7 select_n.196
  18.7 2.7 select_n.200
  23.0 2.6 copy.698
  27.0 7.1 collective-permute-start
  43.6 1.9 collective-permute-start.2
  45.5 3.6 collective-permute-start.3
  49.3 80.1 %all-reduce.5.cloned.1.call-done = bf16[16,12,4,128]{1,0,3,2:T(8,128)(2,1)} async-done(((bf16[16,12,4,128]{1,0,3,2:T(8,128)(2,1)}), bf16[16,12,4,128]{1,0,3,2:T(8,128)(2,1)}) %all-reduce.5.cloned.1.call-update) | async-done | bytes 196624 | tf_op jit(solution)/shard_map/psum | solution.py:75
  132.0 67.8 %all-reduce.7.cloned.1.call-done = bf16[16,12,4,128]{1,0,3,2:T(8,128)(2,1)} async-done(((bf16[16,12,4,128]{1,0,3,2:T(8,128)(2,1)}), bf16[16,12,4,128]{1,0,3,2:T(8,128)(2,1)}) %all-reduce.7.cloned.1.call-update) | async-done | bytes 196624 | tf_op jit(solution)/shard_map/psum | solution.py:75
  199.8 3.0 copy.702
  210.8 3.8 scatter.30
  218.6 18.3 %scatter.31 = bf16[16,12,18,34]{3,0,2,1:T(8,128)(2,1)S(1)} dynamic-update-slice(bf16[16,12,18,34]{3,0,2,1:T(8,128)(2,1)S(1)} %scatter.30, bf16[16,12,18,1]{3,0,2,1:T(8,128)(2,1)S(1)} %copy.707, s32[]{:T(128)} %constant.235.clone.1, s32[]{:T(128)} %constant.235.clone.1, s32[]{:T(128)} %constant.235.clone.1, s32[]{:T(128)} %constant.249.clone.1) | dynamic-update-slice | bytes 13828 | tf_op jit(solution)/shard_map/scatter | solution.py:97
  238.8 161.8 %all-gather.3.cloned.1.call-done = bf16[128,12,18,34]{3,0,2,1:T(8,128)(2,1)} async-done(((bf16[16,12,18,34]{3,0,2,1:T(8,128)(2,1)}), bf16[128,12,18,34]{3,0,2,1:T(8,128)(2,1)}) %all-gather.3.cloned.1.call-update) | async-done | bytes 1880080 | tf_op jit(solution)/shard_map/all_gather | solution.py:151
  400.6 4.7 fusion.20
  414.5 2.0 fusion.18
  416.5 2.6 fusion.37
  421.4 2.3 copy.725
  425.0 1.9 select_n.220
  427.0 1.9 select_n.223
  431.1 2.6 copy.727
  435.0 5.4 collective-permute-start.4
  444.3 5.7 collective-permute-done.5
  451.3 1.9 collective-permute-start.6
  453.3 3.6 collective-permute-start.7
  456.9 73.5 %all-reduce.9.cloned.1.call-done = bf16[16,12,4,128]{1,0,3,2:T(8,128)(2,1)} async-done(((bf16[16,12,4,128]{1,0,3,2:T(8,128)(2,1)}), bf16[16,12,4,128]{1,0,3,2:T(8,128)(2,1)}) %all-reduce.9.cloned.1.call-update) | async-done | bytes 196624 | tf_op jit(solution)/shard_map/psum | solution.py:75
  532.9 67.6 %all-reduce.11.cloned.1.call-done = bf16[16,12,4,128]{1,0,3,2:T(8,128)(2,1)} async-done(((bf16[16,12,4,128]{1,0,3,2:T(8,128)(2,1)}), bf16[16,12,4,128]{1,0,3,2:T(8,128)(2,1)}) %all-reduce.11.cloned.1.call-update) | async-done | bytes 196624 | tf_op jit(solution)/shard_map/psum | solution.py:75
  600.6 3.0 copy.731
  612.2 3.8 scatter.36
  619.4 18.6 %scatter.39 = bf16[16,12,18,34]{3,0,2,1:T(8,128)(2,1)S(1)} dynamic-update-slice(bf16[16,12,18,34]{3,0,2,1:T(8,128)(2,1)S(1)} %scatter.36, bf16[16,12,18,1]{3,0,2,1:T(8,128)(2,1)S(1)} %copy.735, s32[]{:T(128)} %constant.235.clone.1, s32[]{:T(128)} %constant.235.clone.1, s32[]{:T(128)} %constant.235.clone.1, s32[]{:T(128)} %constant.249.clone.1) | dynamic-update-slice | bytes 13828 | tf_op jit(solution)/shard_map/scatter | solution.py:97
  641.7 159.9 %all-gather.5.cloned.1.call-done = bf16[128,12,18,34]{3,0,2,1:T(8,128)(2,1)} async-done(((bf16[16,12,18,34]{3,0,2,1:T(8,128)(2,1)}), bf16[128,12,18,34]{3,0,2,1:T(8,128)(2,1)}) %all-gather.5.cloned.1.call-update) | async-done | bytes 1880080 | tf_op jit(solution)/shard_map/all_gather | solution.py:158
  801.6 4.8 fusion.2
  817.3 2.3 add_convert_fusion
  (203 shorter events, 86.3 us)
Async XLA Ops:
  7.2 393.5 %copy-start = (bf16[3,3,128,128]{3,2,1,0:T(8,128)(2,1)S(1)}, bf16[3,3,128,128]{3,2,1,0:T(8,128)(2,1)}, u32[]{:S(2)}) copy-start(bf16[3,3,128,128]{3,2,1,0:T(8,128)(2,1)} %param.27) | copy-start | bytes 884740
  7.2 122.2 %all-reduce.5.cloned.1.call-start = ((), (), s32[]{:S(2)}) async-start(), calls=%async_computation | async-start | bytes 4194304 | tf_op jit(solution)/shard_map/psum | solution.py:75
  25.7 10.9 %copy-start.15 = (s32[12,4,3]{0,1,2:T(4,128)S(1)}, s32[12,4,3]{0,1,2:T(4,128)}, u32[]{:S(2)}) copy-start(s32[12,4,3]{0,1,2:T(4,128)} %param.28) | copy-start | bytes 1732
  25.7 12.1 %copy-start.24 = (s32[12,4,2]{0,2,1:T(2,128)S(1)}, s32[12,4,2]{0,2,1:T(2,128)}, u32[]{:S(2)}) copy-start(s32[12,4,2]{0,2,1:T(2,128)} %param.29) | copy-start | bytes 1156
  25.7 174.1 %all-reduce.7.cloned.1.call-start = ((), (), s32[]{:S(2)}) async-start(), calls=%async_computation.1 | async-start | bytes 4194304 | tf_op jit(solution)/shard_map/psum | solution.py:75
  27.0 12.4 %collective-permute-start = (bf16[16,12,16,1]{2,0,3,1:T(8,128)(2,1)S(1)}, bf16[16,12,16,1]{2,0,3,1:T(8,128)(2,1)S(1)}, u32[]{:S(2)}, u32[]{:S(2)}) collective-permute-start(bf16[16,12,16,1]{2,0,3,1:T(8,128)(2,1)S(1)} %copy.684), channel_id=1, source_target_pairs={{0,64},{64,128},{128,192},{1,65},{65,129},{129,193},{2,66},{66,130... | collective-permute-start | bytes 18440 | tf_op jit(solution)/shard_map/ppermute | solution.py:16
  35.3 6.0 collective-permute-start.1
  43.6 86.1 %collective-permute-start.2 = (bf16[16,12,1,34]{3,0,1,2:T(8,128)(2,1)S(1)}, bf16[16,12,1,34]{3,0,1,2:T(8,128)(2,1)S(1)}, u32[]{:S(2)}, u32[]{:S(2)}) collective-permute-start(bf16[16,12,1,34]{3,0,1,2:T(8,128)(2,1)S(1)} %get-tuple-element.148), channel_id=1, source_target_pairs={{0,8},{8,16},{16,24},{24,32},{32,40},{40,48},{48,56},{1,9},{9,17},... | collective-permute-start | bytes 39176 | tf_op jit(solution)/shard_map/ppermute | solution.py:16
  45.5 84.2 %collective-permute-start.3 = (bf16[16,12,1,34]{3,0,1,2:T(8,128)(2,1)S(1)}, bf16[16,12,1,34]{3,0,1,2:T(8,128)(2,1)S(1)}, u32[]{:S(2)}, u32[]{:S(2)}) collective-permute-start(bf16[16,12,1,34]{3,0,1,2:T(8,128)(2,1)S(1)} %get-tuple-element.149), channel_id=1, source_target_pairs={{8,0},{16,8},{24,16},{32,24},{40,32},{48,40},{56,48},{9,1},{17,9},... | collective-permute-start | bytes 39176 | tf_op jit(solution)/shard_map/ppermute | solution.py:17
  129.4 271.2 %all-gather.3.cloned.1.call-start = ((), (), s32[]{:S(2)}) async-start(), calls=%async_computation.2 | async-start | bytes 7962624 | tf_op jit(solution)/shard_map/all_gather | solution.py:151
  131.9 71.8 %copy-start.13 = (pred[12]{0:T(512)(128)(4,1)S(1)}, pred[12]{0:T(512)(128)(4,1)}, u32[]{:S(2)}) copy-start(pred[12]{0:T(512)(128)(4,1)} %get-tuple-element.166) | copy-start | bytes 40
  131.9 72.6 %copy-start.11 = (pred[12]{0:T(512)(128)(4,1)S(1)}, pred[12]{0:T(512)(128)(4,1)}, u32[]{:S(2)}) copy-start(pred[12]{0:T(512)(128)(4,1)} %get-tuple-element.164) | copy-start | bytes 40
  131.9 75.5 %copy-start.18 = (pred[12]{0:T(512)(128)(4,1)S(1)}, pred[12]{0:T(512)(128)(4,1)}, u32[]{:S(2)}) copy-start(pred[12]{0:T(512)(128)(4,1)} %get-tuple-element.163) | copy-start | bytes 40
  202.8 4.7 copy-start.9
  202.8 4.8 copy-start.20
  204.7 4.5 copy-start.22
  217.3 21.1 %copy-start.5 = (bf16[16,12,1,1,512]{4,0,3,2,1:T(8,128)(2,1)S(1)}, bf16[16,12,1,1,512]{4,0,3,2,1:T(8,128)(2,1)}, u32[]{:S(2)}) copy-start(bf16[16,12,1,1,512]{4,0,3,2,1:T(8,128)(2,1)} %param.26) | copy-start | bytes 589828
  238.0 292.4 %all-reduce.9.cloned.1.call-start = ((), (), s32[]{:S(2)}) async-start(), calls=%async_computation.3 | async-start | bytes 4194304 | tf_op jit(solution)/shard_map/psum | solution.py:75
  400.6 4.8 copy-start.2
  433.7 166.8 %all-reduce.11.cloned.1.call-start = ((), (), s32[]{:S(2)}) async-start(), calls=%async_computation.4 | async-start | bytes 4194304 | tf_op jit(solution)/shard_map/psum | solution.py:75
  435.0 8.0 collective-permute-start.4
  441.7 8.3 collective-permute-start.5
  451.3 79.4 %collective-permute-start.6 = (bf16[16,12,1,34]{3,0,2,1:T(8,128)(2,1)S(1)}, bf16[16,12,1,34]{3,0,2,1:T(8,128)(2,1)S(1)}, u32[]{:S(2)}, u32[]{:S(2)}) collective-permute-start(bf16[16,12,1,34]{3,0,2,1:T(8,128)(2,1)S(1)} %get-tuple-element.128), channel_id=1, source_target_pairs={{0,8},{8,16},{16,24},{24,32},{32,40},{40,48},{48,56},{1,9},{9,17},... | collective-permute-start | bytes 39176 | tf_op jit(solution)/shard_map/ppermute | solution.py:16
  453.3 78.1 %collective-permute-start.7 = (bf16[16,12,1,34]{3,0,2,1:T(8,128)(2,1)S(1)}, bf16[16,12,1,34]{3,0,2,1:T(8,128)(2,1)}, u32[]{:S(2)}, u32[]{:S(2)}) collective-permute-start(bf16[16,12,1,34]{3,0,2,1:T(8,128)(2,1)S(1)} %get-tuple-element.129), channel_id=1, source_target_pairs={{8,0},{16,8},{24,16},{32,24},{40,32},{48,40},{56,48},{9,1},{17,9},... | collective-permute-start | bytes 39176 | tf_op jit(solution)/shard_map/ppermute | solution.py:17
  530.4 271.2 %all-gather.5.cloned.1.call-start = ((), (), s32[]{:S(2)}) async-start(), calls=%async_computation.5 | async-start | bytes 7962624 | tf_op jit(solution)/shard_map/all_gather | solution.py:158
  532.9 73.6 %copy-start.14 = (pred[12]{0:T(512)(128)(4,1)S(1)}, pred[12]{0:T(512)(128)(4,1)}, u32[]{:S(2)}) copy-start(pred[12]{0:T(512)(128)(4,1)} %get-tuple-element.166) | copy-start | bytes 40
  532.9 73.8 %copy-start.23 = (pred[12]{0:T(512)(128)(4,1)S(1)}, pred[12]{0:T(512)(128)(4,1)}, u32[]{:S(2)}) copy-start(pred[12]{0:T(512)(128)(4,1)} %get-tuple-element.162) | copy-start | bytes 40
  532.9 73.9 %copy-start.12 = (pred[12]{0:T(512)(128)(4,1)S(1)}, pred[12]{0:T(512)(128)(4,1)}, u32[]{:S(2)}) copy-start(pred[12]{0:T(512)(128)(4,1)} %get-tuple-element.164) | copy-start | bytes 40
  532.9 74.1 %copy-start.21 = (pred[12]{0:T(512)(128)(4,1)S(1)}, pred[12]{0:T(512)(128)(4,1)}, u32[]{:S(2)}) copy-start(pred[12]{0:T(512)(128)(4,1)} %get-tuple-element.161) | copy-start | bytes 40
  603.6 5.5 copy-start.19
  603.6 5.6 copy-start.7
  801.6 4.8 copy-start.1
  (7 other events, 8.1 us)
Sparse Core Ops, SparseCore 0:
  25.8 103.5 all-reduce.4
  131.9 67.8 all-reduce.6
  238.1 162.4 all-gather.2
  433.9 96.5 all-reduce.8
  532.6 67.8 all-reduce.10
  639.1 162.4 all-gather.4
